TPU v7x, 256 devices: a whole 4x4x8 slice. The times are simulated.
256 devices in a mesh: blk: 32 (over x, z), leaf: 4 (over y), samp: 2 (over core).
Axes of the slice: x: 4, y: 4, z: 8, core: 2. Of those that a mesh axis runs over, the one named last changes fastest.
Arguments:
- points: float32 [3, 32768], P(None, ('blk', 'leaf')), may hold values from 0 to 64, as said below
- neighbors: int32 [128, 8], P(('blk', 'leaf')), may hold values from -1 to 127, as said below
- omega: float32 [512, 32768], P(None, ('blk', 'leaf')), may hold values from -6 to 6
- observed: float32 [32768], P(('blk', 'leaf')), may hold values from -6 to 6
- prior_draws: float32 [64, 32768], P('samp', ('blk', 'leaf')), may hold values from -6 to 6
Outputs:
- weights: float32 [64, 32768], P('samp', ('blk', 'leaf'))
- residual: float32 [64, 32768], P('samp', ('blk', 'leaf'))
Inputs may be any that keep to these rules, and one draw needn't show every extreme that they name: Block g's points lie in the unit cell with integer corner (cx, cy, cz), where cx // 2 = g // 4 and 0 <= cy, cz < 3. `neighbors`: row g lists in ascending order every block h whose unit cell touches g's (cells at most one apart in every coordinate, the first taken periodic of period 2 * 32), which includes every block with a point within distance 1 of a point of g, followed by -1 in the unused slots; the relation is symmetric, and every listed block has a slab index h // 4 equal to or cyclically next to g // 4.
All inputs are finite; a program needn't handle non-finite values.
Results may differ from a plain program's by a relative error of at most 0.0003.
Values sent between devices are 32-bit elements; how exact they have to be, the bound alone decides.
A program may use at most 64 MiB of HBM per device.

v0:
```python
import jax
import jax.numpy as jnp
from jax import lax
from jax.sharding import PartitionSpec as P

PB = 256
ITERS = 2
support_radius = 0.8
noise_variance = 1.0
sketch_shift = 1.0


def shifted_2(block, axis, distance):
    devices = range(lax.axis_size(axis))
    route = [((i - distance) % len(devices), i) for i in devices]
    return lax.ppermute(block, axis, route)


def wendland(row_points, column_points, period):
    offset = row_points[None, :, :, None] - column_points[:, :, None, :]
    half_period = 0.5 * period
    along_x = jnp.mod(offset[:, 0] + half_period, period) - half_period
    squared = along_x * along_x + offset[:, 1] * offset[:, 1] + offset[:, 2] * offset[:, 2]
    radius = jnp.sqrt(squared) / support_radius
    remain = jnp.maximum(1.0 - radius, 0.0)
    return remain**4 * (4.0 * radius + 1.0)


def high_dot(left, right):
    return jnp.dot(left, right, precision=lax.Precision.HIGHEST, preferred_element_type=jnp.float32)


def shifted(values, offset_by):
    return shifted_2(values, "blk", offset_by)


def beside_all(values):
    slab_values = lax.all_gather(values, "leaf", axis=1, tiled=True)
    return jnp.concatenate([shifted(slab_values, 1), slab_values, shifted(slab_values, -1)], axis=1)


def total(values):
    return lax.psum(values, ("blk", "leaf"))


def lower_solve(factor, values):
    return lax.linalg.triangular_solve(factor, values, left_side=True, lower=True)


def local(points, neighbors, omega, observed, prior_draws):
    blk_dev = neighbors.shape[0]
    cycle_count = lax.axis_size("blk")
    slab_blocks = blk_dev * lax.axis_size("leaf")
    period = 2.0 * cycle_count
    own_slab = lax.axis_index("blk")
    usable = neighbors >= 0
    relative = jnp.mod(neighbors // slab_blocks - own_slab + 1, cycle_count)
    chosen = jnp.where(usable, relative * slab_blocks + jnp.mod(neighbors, slab_blocks), 0)
    usable_weight = usable.astype(jnp.float32)
    reach_points = beside_all(points)
    reach_blocks = reach_points.reshape(3, 3 * slab_blocks, PB).transpose(1, 0, 2)
    row_blocks = points.reshape(3, blk_dev, PB).transpose(1, 0, 2)

    def build_tile(block_index):
        kernel_tile = wendland(row_blocks[block_index], reach_blocks[chosen[block_index]], period)
        return kernel_tile * usable_weight[block_index][:, None, None]

    def apply_kernel(values):
        width = values.shape[0]
        reach = beside_all(values).reshape(width, 3 * slab_blocks, PB)
        picked = jnp.take(reach, chosen[0], axis=1)
        pieces = jnp.einsum("cnj,nij->ci", picked, build_tile(0), precision=lax.Precision.HIGHEST)
        return pieces

    sketch = apply_kernel(omega) + sketch_shift * omega
    core_gram = total(high_dot(omega, sketch.T))
    core_gram = 0.5 * (core_gram + core_gram.T)
    factor = jnp.linalg.cholesky(core_gram)
    basis = lower_solve(factor, sketch)
    basis_gram = total(high_dot(basis, basis.T))
    woodbury = noise_variance * jnp.eye(basis.shape[0], dtype=jnp.float32) + 0.5 * (
        basis_gram + basis_gram.T
    )
    wood_factor = jnp.linalg.cholesky(woodbury)

    def inverse_apply(vectors):
        projected = total(high_dot(basis, vectors.T))
        first_solve = lower_solve(wood_factor, projected)
        solved = lax.linalg.triangular_solve(
            wood_factor, first_solve, left_side=True, lower=True, transpose_a=True
        )
        return (vectors - high_dot(solved.T, basis)) / noise_variance

    rhs = observed[None, :] - prior_draws
    weights = jnp.zeros_like(rhs)
    residual = rhs
    precond = inverse_apply(residual)
    direction = precond
    inner_now = total(jnp.sum(residual * precond, axis=1))
    for step_index in range(ITERS):
        image = apply_kernel(direction) + noise_variance * direction
        step_size = inner_now / total(jnp.sum(direction * image, axis=1))
        weights = weights + step_size[:, None] * direction
        residual = residual - step_size[:, None] * image
        if step_index + 1 < ITERS:
            precond = inverse_apply(residual)
            inner_next = total(jnp.sum(residual * precond, axis=1))
            direction = precond + (inner_next / inner_now)[:, None] * direction
            inner_now = inner_next
    return (weights, residual)


def solution(mesh):
    in_specs = (
        P(None, ("blk", "leaf")),
        P(("blk", "leaf"), None),
        P(None, ("blk", "leaf")),
        P(("blk", "leaf")),
        P("samp", ("blk", "leaf")),
    )
    out_specs = (P("samp", ("blk", "leaf")), P("samp", ("blk", "leaf")))
    return jax.shard_map(local, mesh=mesh, in_specs=in_specs, out_specs=out_specs, check_vma=False)
```

profile of v0, /device:TPU:8, one launch (start us, length us, event | category | flops | bytes accessed | tf_op | source)
XLA Modules:
  0.0 2182.1 jit_solution(1720659250722919533)
XLA Ops:
  9.3 12.3 all_gather.13
  21.6 8.1 collective-permute-start.3
  29.7 15.5 all-gather.2.cloned.1.call-done
  45.2 5.4 collective-permute-start.1
  53.9 2.6 multiply_multiply_fusion
  56.6 39.3 %collective-permute-done.1 = f32[512,1024]{0,1:T(8,128)} collective-permute-done((f32[512,1024]{0,1:T(8,128)}, f32[512,1024]{0,1:T(8,128)}, u32[]{:S(2)}, u32[]{:S(2)}) %collective-permute-start.1) | collective-permute-done | bytes 2097184 | tf_op jit(solution)/shard_map/ppermute | solution.py:16
  95.8 5.5 collective-permute-done
  101.3 5.6 pad_maximum_fusion
  106.9 6.5 copy.13
  113.5 5.6 gather_fusion
  119.0 5.5 fusion.17
  127.7 214.8 %all-reduce.7.cloned.1.call-done = f32[512,512]{1,0:T(8,128)} async-done(((f32[512,512]{1,0:T(8,128)}), f32[512,512]{1,0:T(8,128)}) %all-reduce.7.cloned.1.call-update) | async-done | bytes 1048592 | tf_op jit(solution)/shard_map/psum | solution.py:43
  342.5 2.6 copy.16
  350.6 11.7 cholesky.286
  362.4 9.8 custom-call.35
  374.8 11.7 cholesky.305
  386.6 10.2 custom-call.36
  398.3 11.7 cholesky.326
  410.8 9.8 custom-call.37
  422.1 11.9 cholesky.343
  439.0 11.7 while.9
  442.6 2.3 bitcast_dynamic-update-slice_fusion.4
  445.6 2.3 bitcast_dynamic-update-slice_fusion.4
  450.7 39.3 %custom-call.29 = f32[4,128,128]{1,2,0:T(8,128)S(1)} custom-call(f32[4,128,128]{2,1,0:T(8,128)S(1)} %get-tuple-element.29), custom_call_target="InvertDiagBlocksLowerTriangular" | custom-call | tf_op jit(solution)/shard_map/triangular_solve | solution.py:47
  499.4 218.7 %all-reduce.11.cloned.1.call-done = (f32[512,512]{1,0:T(8,128)}, f32[512,32]{0,1:T(8,128)}) async-done(((f32[512,512]{1,0:T(8,128)}, f32[512,32]{0,1:T(8,128)}), (f32[512,512]{1,0:T(8,128)}, f32[512,32]{0,1:T(8,128)})) %all-reduce.11.cloned.1.call-update) | async-done | bytes 1114128 | tf_op jit(solution)/shard_map/psum | solution.py:43
  718.1 2.6 copy.18
  726.3 11.7 cholesky.358
  738.7 9.8 custom-call.38
  751.8 11.7 cholesky.377
  764.2 10.2 custom-call.39
  776.8 11.7 cholesky.398
  789.3 9.8 custom-call.40
  800.5 11.9 cholesky.415
  817.1 8.5 while.10
  826.3 40.1 %custom-call.42 = f32[4,128,128]{1,2,0:T(8,128)S(1)} custom-call(f32[4,128,128]{2,1,0:T(8,128)} %copy-done.13), custom_call_target="InvertDiagBlocksLowerTriangular" | custom-call | tf_op jit(solution)/shard_map/triangular_solve/custom-call.9 | solution.py:89
  873.7 11.9 all_gather.14
  885.6 2.7 collective-permute-start.5
  888.3 2.5 collective-permute-done.5
  890.8 5.8 collective-permute-done.4
  897.4 2.3 gather_fusion.2
  899.7 4.2 multiply_reduce_fusion.2
  903.9 344.3 %all-reduce.1 = (f32[32]{0:T(128)}, f32[32]{0:T(128)}) all-reduce(f32[32]{0:T(128)} %get-tuple-element.47, f32[32]{0:T(128)S(1)} %get-tuple-element.46), channel_id=1, replica_groups=mesh['blk'=32,'leaf'=4,'samp'=2] {'blk','leaf'}, use_global_device_ids=true, to_apply=%region_12.16 | all-reduce | flops 64 | bytes 512 | tf_op jit(solution)/shard_map/psum | solution.py:43
  1252.6 201.5 %all-reduce.9.cloned.1.call-done = f32[512,32]{0,1:T(8,128)} async-done(((f32[512,32]{0,1:T(8,128)}), f32[512,32]{0,1:T(8,128)}) %all-reduce.9.cloned.1.call-update) | async-done | bytes 65552 | tf_op jit(solution)/shard_map/psum | solution.py:43
  1461.5 342.7 %psum.62 = f32[32]{0:T(128)S(1)} all-reduce(f32[32]{0:T(128)S(1)} %get-tuple-element.101), channel_id=1, replica_groups=mesh['blk'=32,'leaf'=4,'samp'=2] {'blk','leaf'}, use_global_device_ids=true, to_apply=%region_17.22 | all-reduce | flops 32 | bytes 256 | tf_op jit(solution)/shard_map/psum | solution.py:43
  1805.6 12.6 all_gather.15
  1820.3 2.9 collective-permute-done.7
  1823.3 3.7 collective-permute-done.6
  1829.6 345.1 %psum.63 = f32[32]{0:T(128)S(1)} all-reduce(f32[32]{0:T(128)S(1)} %get-tuple-element.103), channel_id=1, replica_groups=mesh['blk'=32,'leaf'=4,'samp'=2] {'blk','leaf'}, use_global_device_ids=true, to_apply=%region_19.24 | all-reduce | flops 32 | bytes 256 | tf_op jit(solution)/shard_map/psum | solution.py:43
  (184 shorter events, 92.0 us)
Async XLA Ops:
  7.2 38.0 %all-gather.2.cloned.1.call-start = ((), (), s32[]{:S(2)}) async-start(), calls=%async_computation | async-start | bytes 2621440 | tf_op jit(solution)/shard_map/all_gather | solution.py:38
  9.3 333.2 %all-reduce.7.cloned.1.call-start = ((), (), s32[]{:S(2)}) async-start(), calls=%async_computation.1 | async-start | bytes 2097152 | tf_op jit(solution)/shard_map/psum | solution.py:43
  21.6 30.4 %collective-permute-start.3 = (f32[3,1024]{1,0:T(4,128)S(1)}, f32[3,1024]{1,0:T(4,128)S(1)}, u32[]{:S(2)}, u32[]{:S(2)}) collective-permute-start(f32[3,1024]{1,0:T(4,128)S(1)} %all_gather.13), channel_id=1, source_target_pairs={{8,0},{16,8},{24,16},{32,24},{40,32},{48,40},{56,48},{64,56},{72,6... | collective-permute-start | bytes 36872 | tf_op jit(solution)/shard_map/ppermute | solution.py:16
  29.7 22.3 %collective-permute-start.2 = (f32[3,1024]{1,0:T(4,128)S(1)}, f32[3,1024]{1,0:T(4,128)S(1)}, u32[]{:S(2)}, u32[]{:S(2)}) collective-permute-start(f32[3,1024]{1,0:T(4,128)S(1)} %all_gather.13), channel_id=1, source_target_pairs={{248,0},{0,8},{8,16},{16,24},{24,32},{32,40},{40,48},{48,56},{56,6... | collective-permute-start | bytes 36872 | tf_op jit(solution)/shard_map/ppermute | solution.py:16
  45.2 50.6 %collective-permute-start.1 = (f32[512,1024]{0,1:T(8,128)}, f32[512,1024]{0,1:T(8,128)}, u32[]{:S(2)}, u32[]{:S(2)}) collective-permute-start(f32[512,1024]{0,1:T(8,128)} %all-gather.2.cloned.1.call-done), channel_id=1, source_target_pairs={{8,0},{16,8},{24,16},{32,24},{40,32},{48,40},{56,48},{64,56},{72,6... | collective-permute-start | bytes 6291464 | tf_op jit(solution)/shard_map/ppermute | solution.py:16
  50.6 50.7 %collective-permute-start = (f32[512,1024]{0,1:T(8,128)}, f32[512,1024]{0,1:T(8,128)}, u32[]{:S(2)}, u32[]{:S(2)}) collective-permute-start(f32[512,1024]{0,1:T(8,128)} %all-gather.2.cloned.1.call-done), channel_id=1, source_target_pairs={{248,0},{0,8},{8,16},{16,24},{24,32},{32,40},{40,48},{48,56},{56,6... | collective-permute-start | bytes 6291464 | tf_op jit(solution)/shard_map/ppermute | solution.py:16
  53.9 47.4 %copy-start.7 = (f32[512,1024]{0,1:T(8,128)S(1)}, f32[512,1024]{0,1:T(8,128)}, u32[]{:S(2)}) copy-start(f32[512,1024]{0,1:T(8,128)} %all-gather.2.cloned.1.call-done) | copy-start | bytes 6291460
  113.5 5.6 copy-start.3
  124.5 0.8 copy-start.1
  127.4 590.7 %all-reduce.11.cloned.1.call-start = ((), (), s32[]{:S(2)}) async-start(), calls=%async_computation.3 | async-start | bytes 2228224 | tf_op jit(solution)/shard_map/psum | solution.py:43
  349.6 1.0 copy-start.5
  439.0 53.8 %copy-start.2 = (f32[512,256]{1,0:T(8,128)S(1)}, f32[512,256]{1,0:T(8,128)}, u32[]{:S(2)}) copy-start(f32[512,256]{1,0:T(8,128)} %copy-done.1) | copy-start | bytes 1572868
  492.4 5.7 copy-start.14
  492.5 5.7 copy-start.17
  492.8 6.6 copy-start.6
  494.4 5.0 copy-start.8
  496.1 222.1 %copy-start.12 = (f32[128,256]{1,0:T(8,128)}, f32[128,256]{1,0:T(8,128)S(1)}, u32[]{:S(2)}) copy-start(f32[128,256]{1,0:T(8,128)S(1)} %fusion.69) | copy-start | bytes 393220
  499.4 954.7 %all-reduce.9.cloned.1.call-start = ((), (), s32[]{:S(2)}) async-start(), calls=%async_computation.2 | async-start | bytes 131072 | tf_op jit(solution)/shard_map/psum | solution.py:43
  725.3 1.0 copy-start.4
  751.1 0.7 copy-start.9
  812.4 3.3 copy-start
  825.6 0.7 copy-start.13
  873.7 17.1 copy-start.10
  885.6 5.2 collective-permute-start.5
  888.3 8.3 collective-permute-start.4
  1249.7 0.6 copy-start.15
  1818.3 356.4 %copy-start.11 = (f32[32,256]{1,0:T(8,128)S(1)}, f32[32,256]{1,0:T(8,128)}, u32[]{:S(2)}) copy-start(f32[32,256]{1,0:T(8,128)} %copy-done.10) | copy-start | bytes 98308
  1818.3 356.4 %copy-start.16 = (f32[32,256]{1,0:T(8,128)S(1)}, f32[32,256]{1,0:T(8,128)}, u32[]{:S(2)}) copy-start(f32[32,256]{1,0:T(8,128)} %copy-done.15) | copy-start | bytes 98308
  1818.3 5.0 collective-permute-start.7
  1818.6 8.3 collective-permute-start.6
Sparse Core Ops, SparseCore 0:
  9.8 35.3 all-gather.1
  127.5 214.8 all-reduce.6
  499.5 218.5 all-reduce.10
  1252.7 201.3 all-reduce.8
where the time goes:
time: 2190 us; the launch traced here: 2180 us
  blocking collectives  1070 us (49%)
  waiting for transfers between devices  710 us (32%)
  other arithmetic  262 us (12%)
  matrix products  51.5 us (2%)
  local copies, waits for them, and re-layouts  51.3 us (2%)
    psum x3, blocking collectives, total(): return lax.psum(values, ('blk', 'leaf'))  1030 us
    psum x3, waiting for transfers between devices, total(): return lax.psum(values, ('blk', 'leaf'))  635 us
    another operation x15, other arithmetic, local(): wood_factor = jnp.linalg.cholesky(woodbury)  79.7 us
    another operation x14, other arithmetic, local(): factor = jnp.linalg.cholesky(core_gram)  79 us
    ppermute x8, waiting for transfers between devices, shifted_2(): return lax.ppermute(block, axis, route)  59.7 us
  transfers between devices with their start and end apart: 12, of which 10 were waited for; matrix products, arithmetic and copies ran while one was open for 0% of the time, Pallas kernels for 0%

commit v1 on v0

--- a/solution.py
+++ b/solution.py
@@ -40,7 +40,7 @@
 
 
 def total(values):
-    return lax.psum(values, ("blk", "leaf"))
+    return lax.psum(lax.psum(values, "blk"), "leaf")
 
 
 def lower_solve(factor, values):

time: 2190 us -> 1340 us (0.61)
  blocking collectives: 1070 us -> 280 us
  waiting for transfers between devices: 710 us -> 649 us
    psum x3 -> x6, blocking collectives: 1030 us -> 245 us  [total(): return lax.psum(lax.psum(values, 'blk'), 'leaf')]
    psum x3 -> x6, waiting for transfers between devices: 635 us -> 574 us  [total(): return lax.psum(lax.psum(values, 'blk'), 'leaf')]
  transfers between devices with their start and end apart: 12 -> 15, of which waited for: 10 -> 13; matrix products, arithmetic and copies ran while one was open for 0% -> 0% of each run, Pallas kernels for 0% -> 0%
where the time goes in v1:
time: 1340 us; the launch traced here: 1330 us
  waiting for transfers between devices  649 us (48%)
  blocking collectives  280 us (21%)
  other arithmetic  262 us (20%)
  matrix products  51.5 us (4%)
  local copies, waits for them, and re-layouts  51.2 us (4%)
  starting transfers between devices  21.5 us (2%)
  between operations  20.1 us (2%)
    psum x6, waiting for transfers between devices, total(): return lax.psum(lax.psum(values, 'blk'), 'leaf')  574 us
    psum x6, blocking collectives, total(): return lax.psum(lax.psum(values, 'blk'), 'leaf')  245 us
    another operation x15, other arithmetic, local(): wood_factor = jnp.linalg.cholesky(woodbury)  79.7 us
    another operation x14, other arithmetic, local(): factor = jnp.linalg.cholesky(core_gram)  79 us
    ppermute x8, waiting for transfers between devices, shifted_2(): return lax.ppermute(block, axis, route)  59.4 us
    another operation x2, other arithmetic, inverse_apply(): lax.linalg.triangular_solve(wood_factor, first_solve, left_side=True, low...  41.5 us
    another operation x3, other arithmetic, lower_solve(): lax.linalg.triangular_solve(factor, values, left_side=True, lower=True)  40.4 us
    all_gather x3, blocking collectives, beside_all(): slab_values = lax.all_gather(values, 'leaf', axis=1, tiled=True)  35.1 us
  transfers between devices with their start and end apart: 15, of which 13 were waited for; matrix products, arithmetic and copies ran while one was open for 0% of the time, Pallas kernels for 0%

profile of v1, /device:TPU:8, one launch (start us, length us, event | category | flops | bytes accessed | tf_op | source)
XLA Modules:
  0.0 1334.5 jit_solution(13698916933156464467)
XLA Ops:
  9.3 12.3 all_gather.13
  21.6 8.1 collective-permute-start.3
  29.7 15.5 %all-gather.2.cloned.1.call-done = f32[512,1024]{0,1:T(8,128)} async-done(((f32[512,256]{0,1:T(8,128)}), f32[512,1024]{0,1:T(8,128)}) %all-gather.2.cloned.1.call-update) | async-done | bytes 2097168 | tf_op jit(solution)/shard_map/all_gather | solution.py:38
  45.2 5.4 collective-permute-start.1
  53.9 2.6 multiply_multiply_fusion
  56.6 39.3 %collective-permute-done.1 = f32[512,1024]{0,1:T(8,128)} collective-permute-done((f32[512,1024]{0,1:T(8,128)}, f32[512,1024]{0,1:T(8,128)}, u32[]{:S(2)}, u32[]{:S(2)}) %collective-permute-start.1) | collective-permute-done | bytes 2097184 | tf_op jit(solution)/shard_map/ppermute | solution.py:16
  95.8 5.5 collective-permute-done
  101.3 5.6 pad_maximum_fusion
  106.9 6.5 copy.13
  113.5 5.6 gather_fusion
  119.0 5.5 fusion.17
  127.5 143.4 %all-reduce.12.cloned.1.call-done = f32[512,512]{1,0:T(8,128)} async-done(((f32[512,512]{1,0:T(8,128)}), f32[512,512]{1,0:T(8,128)}) %all-reduce.12.cloned.1.call-update) | async-done | bytes 1048592 | tf_op jit(solution)/shard_map/psum | solution.py:43
  271.2 49.7 %all-reduce.14.cloned.1.call-done = f32[512,512]{1,0:T(8,128)} async-done(((f32[512,512]{1,0:T(8,128)}), f32[512,512]{1,0:T(8,128)}) %all-reduce.14.cloned.1.call-update) | async-done | bytes 1048592 | tf_op jit(solution)/shard_map/psum | solution.py:43
  328.9 11.7 cholesky.286
  340.7 9.8 custom-call.35
  353.2 11.7 cholesky.305
  364.9 10.2 custom-call.36
  376.7 11.7 cholesky.326
  389.1 9.8 custom-call.37
  400.4 11.9 cholesky.343
  417.3 11.7 while.9
  429.0 39.3 %custom-call.29 = f32[4,128,128]{1,2,0:T(8,128)S(1)} custom-call(f32[4,128,128]{2,1,0:T(8,128)S(1)} %get-tuple-element.29), custom_call_target="InvertDiagBlocksLowerTriangular" | custom-call | tf_op jit(solution)/shard_map/triangular_solve | solution.py:47
  477.8 151.8 %all-reduce.20.cloned.1.call-done = (f32[512,512]{1,0:T(8,128)}, f32[512,32]{0,1:T(8,128)}) async-done(((f32[512,512]{1,0:T(8,128)}, f32[512,32]{0,1:T(8,128)}), (f32[512,512]{1,0:T(8,128)}, f32[512,32]{0,1:T(8,128)})) %all-reduce.20.cloned.1.call-update) | async-done | bytes 1114128 | tf_op jit(solution)/shard_map/psum | solution.py:43
  629.6 50.0 %all-reduce.22.cloned.1.call-done = (f32[512,512]{1,0:T(8,128)}, f32[512,32]{0,1:T(8,128)}) async-done(((f32[512,512]{1,0:T(8,128)}, f32[512,32]{0,1:T(8,128)}), (f32[512,512]{1,0:T(8,128)}, f32[512,32]{0,1:T(8,128)})) %all-reduce.22.cloned.1.call-update) | async-done | bytes 1114128 | tf_op jit(solution)/shard_map/psum | solution.py:43
  687.7 11.7 cholesky.358
  700.1 9.8 custom-call.38
  713.2 11.7 cholesky.377
  725.6 10.2 custom-call.39
  738.3 11.7 cholesky.398
  750.8 9.8 custom-call.40
  762.0 11.9 cholesky.415
  778.6 8.5 while.10
  787.8 40.1 %custom-call.42 = f32[4,128,128]{1,2,0:T(8,128)S(1)} custom-call(f32[4,128,128]{2,1,0:T(8,128)} %copy-done.13), custom_call_target="InvertDiagBlocksLowerTriangular" | custom-call | tf_op jit(solution)/shard_map/triangular_solve/custom-call.9 | solution.py:89
  835.2 12.0 all_gather.14
  847.2 5.5 collective-permute-start.5
  855.2 5.8 collective-permute-done.4
  864.0 4.1 multiply_reduce_fusion.2
  868.1 70.2 %all-reduce.1 = (f32[32]{0:T(128)}, f32[32]{0:T(128)}) all-reduce(f32[32]{0:T(128)} %get-tuple-element.47, f32[32]{0:T(128)S(1)} %get-tuple-element.46), channel_id=1, replica_groups=mesh['blk'=32,'leaf'=4,'samp'=2] {'blk'}, use_global_device_ids=true, to_apply=%region_15.19 | all-reduce | flops 64 | bytes 512 | tf_op jit(solution)/shard_map/psum | solution.py:43
  938.3 9.7 all-reduce.3
  952.5 133.6 %all-reduce.16.cloned.1.call-done = f32[512,32]{0,1:T(8,128)} async-done(((f32[512,32]{0,1:T(8,128)}), f32[512,32]{0,1:T(8,128)}) %all-reduce.16.cloned.1.call-update) | async-done | bytes 65552 | tf_op jit(solution)/shard_map/psum | solution.py:43
  1086.1 45.4 %all-reduce.18.cloned.1.call-done = f32[512,32]{0,1:T(8,128)} async-done(((f32[512,32]{0,1:T(8,128)}), f32[512,32]{0,1:T(8,128)}) %all-reduce.18.cloned.1.call-update) | async-done | bytes 65552 | tf_op jit(solution)/shard_map/psum | solution.py:43
  1138.9 75.1 %psum.124 = f32[32]{0:T(128)S(1)} all-reduce(f32[32]{0:T(128)S(1)} %get-tuple-element.105), channel_id=1, replica_groups=mesh['blk'=32,'leaf'=4,'samp'=2] {'blk'}, use_global_device_ids=true, to_apply=%region_23.28 | all-reduce | flops 32 | bytes 256 | tf_op jit(solution)/shard_map/psum | solution.py:43
  1213.9 9.4 psum.125
  1224.8 10.8 all_gather.15
  1237.7 2.9 collective-permute-done.7
  1240.6 3.4 collective-permute-done.6
  1246.7 69.6 %psum.126 = f32[32]{0:T(128)S(1)} all-reduce(f32[32]{0:T(128)S(1)} %get-tuple-element.107), channel_id=1, replica_groups=mesh['blk'=32,'leaf'=4,'samp'=2] {'blk'}, use_global_device_ids=true, to_apply=%region_26.31 | all-reduce | flops 32 | bytes 256 | tf_op jit(solution)/shard_map/psum | solution.py:43
  1316.3 10.5 psum.127
  (196 shorter events, 106.5 us)
Async XLA Ops:
  7.2 38.0 %all-gather.2.cloned.1.call-start = ((), (), s32[]{:S(2)}) async-start(), calls=%async_computation | async-start | bytes 2621440 | tf_op jit(solution)/shard_map/all_gather | solution.py:38
  9.3 261.6 %all-reduce.12.cloned.1.call-start = ((), (), s32[]{:S(2)}) async-start(), calls=%async_computation.1 | async-start | bytes 2097152 | tf_op jit(solution)/shard_map/psum | solution.py:43
  21.6 30.4 %collective-permute-start.3 = (f32[3,1024]{1,0:T(4,128)S(1)}, f32[3,1024]{1,0:T(4,128)S(1)}, u32[]{:S(2)}, u32[]{:S(2)}) collective-permute-start(f32[3,1024]{1,0:T(4,128)S(1)} %all_gather.13), channel_id=1, source_target_pairs={{8,0},{16,8},{24,16},{32,24},{40,32},{48,40},{56,48},{64,56},{72,6... | collective-permute-start | bytes 36872 | tf_op jit(solution)/shard_map/ppermute | solution.py:16
  29.7 22.3 %collective-permute-start.2 = (f32[3,1024]{1,0:T(4,128)S(1)}, f32[3,1024]{1,0:T(4,128)S(1)}, u32[]{:S(2)}, u32[]{:S(2)}) collective-permute-start(f32[3,1024]{1,0:T(4,128)S(1)} %all_gather.13), channel_id=1, source_target_pairs={{248,0},{0,8},{8,16},{16,24},{24,32},{32,40},{40,48},{48,56},{56,6... | collective-permute-start | bytes 36872 | tf_op jit(solution)/shard_map/ppermute | solution.py:16
  45.2 50.6 %collective-permute-start.1 = (f32[512,1024]{0,1:T(8,128)}, f32[512,1024]{0,1:T(8,128)}, u32[]{:S(2)}, u32[]{:S(2)}) collective-permute-start(f32[512,1024]{0,1:T(8,128)} %all-gather.2.cloned.1.call-done), channel_id=1, source_target_pairs={{8,0},{16,8},{24,16},{32,24},{40,32},{48,40},{56,48},{64,56},{72,6... | collective-permute-start | bytes 6291464 | tf_op jit(solution)/shard_map/ppermute | solution.py:16
  50.6 50.7 %collective-permute-start = (f32[512,1024]{0,1:T(8,128)}, f32[512,1024]{0,1:T(8,128)}, u32[]{:S(2)}, u32[]{:S(2)}) collective-permute-start(f32[512,1024]{0,1:T(8,128)} %all-gather.2.cloned.1.call-done), channel_id=1, source_target_pairs={{248,0},{0,8},{8,16},{16,24},{24,32},{32,40},{40,48},{48,56},{56,6... | collective-permute-start | bytes 6291464 | tf_op jit(solution)/shard_map/ppermute | solution.py:16
  53.9 47.4 %copy-start.7 = (f32[512,1024]{0,1:T(8,128)S(1)}, f32[512,1024]{0,1:T(8,128)}, u32[]{:S(2)}) copy-start(f32[512,1024]{0,1:T(8,128)} %all-gather.2.cloned.1.call-done) | copy-start | bytes 6291460
  113.5 5.6 copy-start.3
  124.5 0.8 copy-start.1
  127.4 193.4 %all-reduce.14.cloned.1.call-start = ((), (), s32[]{:S(2)}) async-start(), calls=%async_computation.2 | async-start | bytes 2097152 | tf_op jit(solution)/shard_map/psum | solution.py:43
  270.9 358.6 %all-reduce.20.cloned.1.call-start = ((), (), s32[]{:S(2)}) async-start(), calls=%async_computation.5 | async-start | bytes 2228224 | tf_op jit(solution)/shard_map/psum | solution.py:43
  327.9 1.0 copy-start.5
  417.3 53.8 %copy-start.2 = (f32[512,256]{1,0:T(8,128)S(1)}, f32[512,256]{1,0:T(8,128)}, u32[]{:S(2)}) copy-start(f32[512,256]{1,0:T(8,128)} %copy-done.1) | copy-start | bytes 1572868
  470.8 5.7 copy-start.14
  470.8 5.7 copy-start.17
  471.1 6.6 copy-start.6
  472.7 5.0 copy-start.8
  474.4 155.2 %copy-start.12 = (f32[128,256]{1,0:T(8,128)}, f32[128,256]{1,0:T(8,128)S(1)}, u32[]{:S(2)}) copy-start(f32[128,256]{1,0:T(8,128)S(1)} %fusion.69) | copy-start | bytes 393220
  477.7 201.9 %all-reduce.22.cloned.1.call-start = ((), (), s32[]{:S(2)}) async-start(), calls=%async_computation.6 | async-start | bytes 2228224 | tf_op jit(solution)/shard_map/psum | solution.py:43
  629.6 456.5 %all-reduce.16.cloned.1.call-start = ((), (), s32[]{:S(2)}) async-start(), calls=%async_computation.3 | async-start | bytes 131072 | tf_op jit(solution)/shard_map/psum | solution.py:43
  686.7 1.0 copy-start.4
  712.6 0.7 copy-start.9
  773.9 3.3 copy-start
  787.1 0.7 copy-start.13
  835.2 20.0 %copy-start.10 = (f32[32,256]{1,0:T(8,128)}, f32[32,256]{1,0:T(8,128)S(1)}, u32[]{:S(2)}) copy-start(f32[32,256]{1,0:T(8,128)S(1)} %convolution_subtract_fusion.10) | copy-start | bytes 98308
  847.2 8.0 collective-permute-start.5
  852.7 8.3 collective-permute-start.4
  949.5 0.6 copy-start.15
  952.4 179.0 %all-reduce.18.cloned.1.call-start = ((), (), s32[]{:S(2)}) async-start(), calls=%async_computation.4 | async-start | bytes 131072 | tf_op jit(solution)/shard_map/psum | solution.py:43
  1235.6 91.2 %copy-start.11 = (f32[32,256]{1,0:T(8,128)S(1)}, f32[32,256]{1,0:T(8,128)}, u32[]{:S(2)}) copy-start(f32[32,256]{1,0:T(8,128)} %copy-done.10) | copy-start | bytes 98308
  1235.6 91.2 %copy-start.16 = (f32[32,256]{1,0:T(8,128)S(1)}, f32[32,256]{1,0:T(8,128)}, u32[]{:S(2)}) copy-start(f32[32,256]{1,0:T(8,128)} %copy-done.15) | copy-start | bytes 98308
  1235.6 5.0 collective-permute-start.7
  1235.6 8.4 collective-permute-start.6
Sparse Core Ops, SparseCore 0:
  9.8 35.3 all-gather.1
  127.5 143.3 all-reduce.11
  273.3 47.5 all-reduce.13
  477.8 151.6 all-reduce.19
  632.0 47.5 all-reduce.21
  952.6 133.4 all-reduce.15
  1088.4 43.0 all-reduce.17
